TPU v7x, 256 devices: a whole 4x4x8 slice. The times are simulated.
256 devices in a mesh: dp: 8 (over x, core), cut: 32 (over y, z).
Axes of the slice: x: 4, y: 4, z: 8, core: 2. Of those that a mesh axis runs over, the one named last changes fastest.
Arguments:
- node_feat: bfloat16 [128, 262144], P(None, ('dp', 'cut')), parts along dimension 1, may hold values from -6 to 6
- edge_feat: bfloat16 [128, 1048576], P(None, ('dp', 'cut')), parts along dimension 1, may hold values from -6 to 6
- route: int32 [256, 32, 128], P(('dp', 'cut')), parts along dimension 0, may hold values from 0 to 1023, as said below
- block_tile: int32 [8192, 2], P(('dp', 'cut')), parts along dimension 0, may hold values from 0 to 39
- block_offset: int32 [8192, 2, 128], P(('dp', 'cut')), parts along dimension 0, may hold values from 0 to 127
- block_count: int32 [8192], P(('dp', 'cut')), parts along dimension 0, may hold values from 1 to 128, as said below
- w_edge1: bfloat16 [128, 384], replicated, may hold values from -0.3125 to 0.3125
- bias_edge1: float32 [128], replicated, may hold values from -3 to 3
- w_edge2: bfloat16 [128, 128], replicated, may hold values from -0.5 to 0.5
- gain_edge: float32 [128], replicated, may hold values from 0.1 to 1.9
- shift_edge: float32 [128], replicated, may hold values from -3 to 3
- w_node1: bfloat16 [128, 256], replicated, may hold values from -0.375 to 0.375
- bias_node1: float32 [128], replicated, may hold values from -3 to 3
- w_node2: bfloat16 [128, 128], replicated, may hold values from -0.5 to 0.5
- gain_node: float32 [128], replicated, may hold values from 0.1 to 1.9
- shift_node: float32 [128], replicated, may hold values from -3 to 3
- node_cot: bfloat16 [128, 262144], P(None, ('dp', 'cut')), parts along dimension 1, may hold values from -6 to 6
Outputs:
- node_out: bfloat16 [128, 262144], P(None, ('dp', 'cut')), parts along dimension 1
- node_grad: float32 [128, 262144], P(None, ('dp', 'cut')), parts along dimension 1
- edge_grad: bfloat16 [128, 1048576], P(None, ('dp', 'cut')), parts along dimension 1
- param_grad: float32 [923648], P('dp'), parts along dimension 0
There are 8 independent parts, one for each index of `dp`. A program takes and returns all parts, laid end to end along the dimension named above; an argument that names none is the same for every part. Nothing has to cross between parts.
Inputs may be any that keep to these rules, and one draw needn't show every extreme that they name: route[c, p, :] holds 128 distinct master rows of partition p. `block_count`: the first block of each partition is full.
All inputs are finite; a program needn't handle non-finite values.
Results may differ from a plain program's by a relative error of at most 0.024.
Values may be sent and summed in bfloat16 or wider, within the bound.
No kernel may reach another device: no remote copies, remote signals or barrier semaphores. Data moves between devices by JAX's collectives and lax.ppermute only.
A program may use at most 128 MiB of HBM per device.

v0:
```python
import math
import jax
import jax.numpy as jnp
from jax import lax
from jax.sharding import PartitionSpec as P


def silu_slope(values):
    sigmoid_val = jax.nn.sigmoid(values)
    return sigmoid_val * (1.0 + values * (1.0 - sigmoid_val))


def layer_norm(values):
    centred = values - jnp.mean(values, axis=0, keepdims=True)
    inverse = lax.rsqrt(jnp.mean(centred * centred, axis=0, keepdims=True) + 1e-05)
    return (centred * inverse, inverse)


def norm_back(upstream, normed, inverse, gain_vec):
    scaled = upstream * gain_vec[:, None]
    return inverse * (
        scaled
        - jnp.mean(scaled, axis=0, keepdims=True)
        - normed * jnp.mean(scaled * normed, axis=0, keepdims=True)
    )


def row_contract(left, right):
    return lax.dot_general(
        left, right, (((1,), (1,)), ((), ())), preferred_element_type=jnp.float32
    )


def lead_contract(weight, values):
    return lax.dot_general(
        weight, values, (((0,), (0,)), ((), ())), preferred_element_type=jnp.float32
    )


def per_device(
    node_feat,
    edge_feat,
    route,
    block_tile,
    block_offset,
    block_count,
    w_edge1,
    bias_edge1,
    w_edge2,
    gain_edge,
    shift_edge,
    w_node1,
    bias_node1,
    w_node2,
    gain_node,
    shift_node,
    node_cot,
):
    latent = node_feat.shape[0]
    masters = node_feat.shape[1]
    peer_count = lax.axis_size("cut")
    total_nodes = masters * peer_count
    total_edges = edge_feat.shape[1] * peer_count
    mirror_index = lax.all_to_all(route[0], "cut", split_axis=0, concat_axis=0, tiled=True).reshape(
        -1
    )

    def fetch_mirrors(master_part):
        outgoing = jnp.take(master_part, mirror_index, axis=1)
        result = lax.all_to_all(outgoing, "cut", split_axis=1, concat_axis=1, tiled=True)
        return result

    def reduce_mirrors(master_part, mirror_part):
        returned = lax.all_to_all(
            mirror_part.astype(jnp.bfloat16), "cut", split_axis=1, concat_axis=1, tiled=True
        ).astype(mirror_part.dtype)
        result = master_part.at[:, mirror_index].add(returned)
        return result

    columns = 128 * block_tile[:, :, None] + block_offset
    send_cols = columns[:, 0, :].reshape(-1)
    recv_cols = columns[:, 1, :].reshape(-1)
    live_mask = (
        (jnp.arange(block_offset.shape[2], dtype=jnp.int32)[None, :] < block_count[:, None])
        .reshape(-1)
        .astype(jnp.float32)
    )
    node_table = jnp.concatenate([node_feat, fetch_mirrors(node_feat)], axis=1)
    local_width = node_table.shape[1]
    stacked = jnp.concatenate(
        [
            edge_feat,
            jnp.take(node_table, send_cols, axis=1),
            jnp.take(node_table, recv_cols, axis=1),
        ],
        axis=0,
    )
    edge_pre = jnp.dot(w_edge1, stacked, preferred_element_type=jnp.float32) + bias_edge1[:, None]
    edge_hidden = jax.nn.silu(edge_pre).astype(jnp.bfloat16)
    edge_post = jnp.dot(w_edge2, edge_hidden, preferred_element_type=jnp.float32)
    edge_normed, edge_inv = layer_norm(edge_post)
    message = (gain_edge[:, None] * edge_normed + shift_edge[:, None]) * live_mask[None, :]
    local_sums = jnp.zeros((latent, local_width), jnp.float32).at[:, recv_cols].add(message)
    aggregate = reduce_mirrors(local_sums[:, :masters], local_sums[:, masters:])
    agg_low = aggregate.astype(jnp.bfloat16)
    node_input = jnp.concatenate([node_feat, agg_low], axis=0)
    node_pre = (
        jnp.dot(w_node1, node_input, preferred_element_type=jnp.float32) + bias_node1[:, None]
    )
    node_hidden = jax.nn.silu(node_pre).astype(jnp.bfloat16)
    node_post = jnp.dot(w_node2, node_hidden, preferred_element_type=jnp.float32)
    node_normed, node_inv = layer_norm(node_post)
    node_out = (
        node_feat.astype(jnp.float32) + gain_node[:, None] * node_normed + shift_node[:, None]
    ).astype(jnp.bfloat16)
    upstream = node_cot.astype(jnp.float32)
    grad_gain_node = jnp.sum(upstream * node_normed, axis=1)
    grad_shift_node = jnp.sum(upstream, axis=1)
    grad_node_post = norm_back(upstream, node_normed, node_inv, gain_node).astype(jnp.bfloat16)
    grad_w_node2 = row_contract(grad_node_post, node_hidden)
    grad_node_full = lead_contract(w_node2, grad_node_post) * silu_slope(node_pre)
    grad_node_pre = grad_node_full.astype(jnp.bfloat16)
    grad_w_node1 = row_contract(grad_node_pre, node_input)
    grad_bias_node1 = jnp.sum(grad_node_full, axis=1)
    node_direct = lead_contract(w_node1[:, :latent], grad_node_pre)
    grad_agg = lead_contract(w_node1[:, latent:], grad_node_pre).astype(jnp.bfloat16)
    node_vec = jnp.concatenate(
        [
            grad_w_node1.reshape(-1),
            grad_bias_node1,
            grad_w_node2.reshape(-1),
            grad_gain_node,
            grad_shift_node,
        ]
    )
    agg_table = jnp.concatenate([grad_agg, fetch_mirrors(grad_agg)], axis=1)
    grad_message = jnp.take(agg_table, recv_cols, axis=1).astype(jnp.float32) * live_mask[None, :]
    grad_gain_edge = jnp.sum(grad_message * edge_normed, axis=1)
    grad_shift_edge = jnp.sum(grad_message, axis=1)
    grad_edge_post = norm_back(grad_message, edge_normed, edge_inv, gain_edge).astype(jnp.bfloat16)
    grad_w_edge2 = row_contract(grad_edge_post, edge_hidden)
    grad_edge_full = lead_contract(w_edge2, grad_edge_post) * silu_slope(edge_pre)
    grad_edge_pre = grad_edge_full.astype(jnp.bfloat16)
    grad_w_edge1 = row_contract(grad_edge_pre, stacked)
    grad_bias_edge1 = jnp.sum(grad_edge_full, axis=1)
    edge_grad = lead_contract(w_edge1[:, :latent], grad_edge_pre).astype(jnp.bfloat16)
    grad_send = lead_contract(w_edge1[:, latent : 2 * latent], grad_edge_pre)
    grad_recv = lead_contract(w_edge1[:, 2 * latent :], grad_edge_pre)
    grad_table = (
        jnp.zeros((latent, local_width), jnp.float32)
        .at[:, send_cols]
        .add(grad_send)
        .at[:, recv_cols]
        .add(grad_recv)
    )
    node_grad = (
        upstream + node_direct + reduce_mirrors(grad_table[:, :masters], grad_table[:, masters:])
    )
    edge_vec = jnp.concatenate(
        [
            grad_w_edge1.reshape(-1),
            grad_bias_edge1,
            grad_w_edge2.reshape(-1),
            grad_gain_edge,
            grad_shift_edge,
        ]
    )
    summed = lax.psum(jnp.concatenate([edge_vec, node_vec]).astype(jnp.bfloat16), "cut").astype(
        jnp.float32
    )
    edge_summed = summed[: edge_vec.shape[0]]
    node_summed = summed[edge_vec.shape[0] :]
    param_grad = jnp.concatenate(
        [edge_summed / math.sqrt(total_edges), node_summed / math.sqrt(total_nodes)]
    )
    return (node_out, node_grad, edge_grad, param_grad)


def solution(mesh):
    in_specs = (
        P(None, ("dp", "cut")),
        P(None, ("dp", "cut")),
        P(("dp", "cut"), None, None),
        P(("dp", "cut"), None),
        P(("dp", "cut"), None, None),
        P(("dp", "cut")),
        P(),
        P(),
        P(),
        P(),
        P(),
        P(),
        P(),
        P(),
        P(),
        P(),
        P(None, ("dp", "cut")),
    )
    out_specs = (P(None, ("dp", "cut")), P(None, ("dp", "cut")), P(None, ("dp", "cut")), P("dp"))
    return jax.shard_map(
        per_device, mesh=mesh, in_specs=in_specs, out_specs=out_specs, check_vma=False
    )
```

profile of v0, /device:TPU:2, one launch (start us, length us, event | category | flops | bytes accessed | tf_op | source)
XLA Modules:
  0.0 506.6 jit_solution(10482661762203878273)
XLA Ops:
  7.2 11.5 %all-to-all-start = ((s32[32,1,128]{2,1,0:T(1,128)}), s32[32,1,128]{2,1,0:T(1,128)S(1)}, u32[]{:S(2)}, u32[]{:S(2)}) async-start(s32[32,1,128]{2,1,0:T(1,128)} %bitcast.144), calls=%async_computation | async-start | bytes 32768 | tf_op jit(solution)/shard_map/all_to_all | solution.py:64
  18.7 0.7 broadcast_multiply_fusion.6
  19.5 0.9 broadcast_add_fusion
  20.3 1.1 copy.38
  21.4 7.0 %all-to-all-done = s32[32,1,128]{2,1,0:T(1,128)S(1)} async-done(((s32[32,1,128]{2,1,0:T(1,128)}), s32[32,1,128]{2,1,0:T(1,128)S(1)}, u32[]{:S(2)}, u32[]{:S(2)}) %all-to-all-start) | async-done | bytes 16416 | tf_op jit(solution)/shard_map/all_to_all | solution.py:64
  28.4 12.1 %gather_fusion = bf16[4096,128]{1,0:T(8,128)(2,1)S(1)} fusion(bf16[128,1024]{0,1:T(8,128)(2,1)S(1)} %copy.38, s32[4096]{0:T(1024)S(1)} %fusion.48), kind=kCustom, calls=%fused_computation.clone | custom fusion | bytes 2113536 | tf_op jit(solution)/shard_map/jit(_take)/gather | solution.py:69
  40.6 2.9 broadcast_select_fusion.1
  43.5 3.9 all-to-all-start.1
  47.5 1.3 copy.36
  48.9 0.6 compare_select_fusion
  49.6 25.4 %all-to-all-done.1 = bf16[128,32,128]{0,2,1:T(8,128)(2,1)S(1)} async-done(((bf16[128,32,128]{0,2,1:T(8,128)(2,1)}), bf16[128,32,128]{0,2,1:T(8,128)(2,1)S(1)}, u32[]{:S(2)}, u32[]{:S(2)}) %all-to-all-start.1) | async-done | bytes 1048608 | tf_op jit(solution)/shard_map/all_to_all | solution.py:70
  75.1 12.1 %gather_fusion.1 = bf16[4096,128]{1,0:T(8,128)(2,1)S(1)} fusion(bf16[128,5120]{0,1:T(8,128)(2,1)S(1)} %pad_maximum_fusion.1, s32[4096]{0:T(1024)S(1)} %fusion.49), kind=kCustom, calls=%fused_computation.1.clone | custom fusion | bytes 2113536 | tf_op jit(solution)/shard_map/jit(_take)/gather | solution.py:93
  87.2 15.0 %gather_fusion.2 = bf16[4096,128]{1,0:T(8,128)(2,1)} fusion(bf16[128,5120]{0,1:T(8,128)(2,1)S(1)} %pad_maximum_fusion.1, s32[4096]{0:T(1024)S(1)} %fusion.50), kind=kCustom, calls=%fused_computation.3.clone | custom fusion | bytes 2113536 | tf_op jit(solution)/shard_map/jit(_take)/gather | solution.py:94
  102.3 3.1 select_bitcast_fusion
  105.4 2.3 multiply_convert_fusion
  107.7 0.4 fusion.60
  108.7 0.8 copy-done.1
  109.5 0.4 fusion.7
  109.9 1.8 copy.37
  111.8 23.3 %scatter_custom_fusion = f32[128,5120]{0,1:T(8,128)S(1)} fusion(s32[4096]{0:T(1024)S(1)} %bitcast.142, f32[4096,128]{1,0:T(8,128)} %copy.37, f32[]{:T(128)} %constant.26.clone.1), kind=kCustom, calls=%fused_computation.47 | custom fusion | flops 524288 | bytes 2621952 | tf_op jit(solution)/shard_map/scatter-add | solution.py:103
  135.1 1.1 slice.89
  136.2 5.1 %all-to-all-start.2 = ((bf16[128,32,128]{0,2,1:T(8,128)(2,1)}), bf16[128,32,128]{0,2,1:T(8,128)(2,1)}, u32[]{:S(2)}, u32[]{:S(2)}) async-start(bf16[128,32,128]{0,2,1:T(8,128)(2,1)} %bitcast.134), calls=%async_computation.2 | async-start | bytes 2097152 | tf_op jit(solution)/shard_map/all_to_all | solution.py:74
  141.4 27.5 %all-to-all-done.2 = bf16[128,32,128]{0,2,1:T(8,128)(2,1)} async-done(((bf16[128,32,128]{0,2,1:T(8,128)(2,1)}), bf16[128,32,128]{0,2,1:T(8,128)(2,1)}, u32[]{:S(2)}, u32[]{:S(2)}) %all-to-all-start.2) | async-done | bytes 1048608 | tf_op jit(solution)/shard_map/all_to_all | solution.py:74
  168.9 23.1 %scatter_custom_fusion.1 = f32[128,1024]{0,1:T(8,128)S(1)} fusion(f32[128,1024]{0,1:T(8,128)S(1)} %slice.66, s32[4096]{0:T(1024)S(1)} %bitcast.145, bf16[128,4096]{0,1:T(8,128)(2,1)} %bitcast.39), kind=kCustom, calls=%fused_computation.22 | custom fusion | flops 1048576 | bytes 1572864 | tf_op jit(solution)/shard_map/scatter-add | solution.py:77
  192.2 1.2 multiply_convert_fusion.1
  193.8 0.8 fusion.37
  194.6 1.0 fusion.35
  195.6 0.9 fusion.62
  196.7 12.1 %gather_fusion.3 = bf16[4096,128]{1,0:T(8,128)(2,1)S(1)} fusion(bf16[128,1024]{0,1:T(8,128)(2,1)S(1)} %fusion.25, s32[4096]{0:T(1024)S(1)} %fusion.48), kind=kCustom, calls=%fused_computation.2.clone | custom fusion | bytes 2113536 | tf_op jit(solution)/shard_map/jit(_take)/gather | solution.py:69
  208.8 2.9 broadcast_select_fusion
  211.7 5.0 all-to-all-start.3
  216.7 0.7 reduce.4
  217.8 0.8 fusion.29
  218.6 25.7 %all-to-all-done.3 = bf16[128,32,128]{0,2,1:T(8,128)(2,1)S(1)} async-done(((bf16[128,32,128]{0,2,1:T(8,128)(2,1)}), bf16[128,32,128]{0,2,1:T(8,128)(2,1)S(1)}, u32[]{:S(2)}, u32[]{:S(2)}) %all-to-all-start.3) | async-done | bytes 1048608 | tf_op jit(solution)/shard_map/all_to_all | solution.py:70
  244.4 15.0 %gather_fusion.4 = bf16[4096,128]{1,0:T(8,128)(2,1)} fusion(bf16[128,5120]{0,1:T(8,128)(2,1)S(1)} %pad_maximum_fusion.2, s32[4096]{0:T(1024)S(1)} %copy-done.18), kind=kCustom, calls=%fused_computation.4.clone | custom fusion | bytes 2113536 | tf_op jit(solution)/shard_map/jit(_take)/gather | solution.py:137
  259.5 1.6 copy.40
  261.4 2.5 fusion.12
  263.9 0.7 fusion.11
  264.6 0.5 copy-done.4
  265.1 0.4 fusion.28
  265.5 1.2 copy-done.41
  266.7 1.5 fusion.58
  268.2 0.3 copy-done.15
  268.5 1.4 fusion.26
  269.9 1.4 fusion.2
  271.3 1.8 fusion.42
  273.1 1.7 fusion.44
  274.8 23.3 %scatter_custom_fusion.2 = f32[128,5120]{0,1:T(8,128)S(1)} fusion(s32[4096]{0:T(1024)} %bitcast.147, f32[4096,128]{1,0:T(8,128)} %fusion.44, f32[]{:T(128)} %constant.26.clone.1), kind=kCustom, calls=%fused_computation.45 | custom fusion | flops 524288 | bytes 2621952 | tf_op jit(solution)/shard_map/scatter-add | solution.py:152
  298.1 23.8 %scatter_fusion = f32[128,5120]{0,1:T(8,128)S(1)} fusion(f32[128,5120]{0,1:T(8,128)S(1)} %scatter_custom_fusion.2, s32[4096]{0:T(1024)S(1)} %bitcast.143, f32[4096,128]{1,0:T(8,128)} %fusion.42), kind=kCustom, calls=%fused_computation.8 | custom fusion | flops 524288 | bytes 6307840 | tf_op jit(solution)/shard_map/scatter-add | solution.py:154
  322.0 1.1 slice.88
  323.1 1.0 reshape.207
  324.1 0.8 dynamic-update-slice.1
  324.9 0.5 dynamic-update-slice.2
  326.0 0.8 dynamic-update-slice.5
  326.8 0.8 dynamic-update-slice.6
  327.6 1.1 dynamic-update-slice.7
  329.1 0.7 copy-done.16
  329.9 2.3 copy.44
  332.8 5.0 all-to-all-start.4
  337.8 136.4 %all-reduce.2.cloned.1.call-done = bf16[115456]{0:T(1024)(128)(2,1)} async-done(((bf16[115456]{0:T(1024)(128)(2,1)}), bf16[115456]{0:T(1024)(128)(2,1)}) %all-reduce.2.cloned.1.call-update) | async-done | bytes 230928 | tf_op jit(solution)/shard_map/psum | solution.py:168
  474.2 1.0 convert_element_type.94
  475.3 0.8 pad_maximum_fusion.8
  476.1 22.7 %scatter_custom_fusion.4 = f32[128,1024]{0,1:T(8,128)S(1)} fusion(f32[128,1024]{0,1:T(8,128)S(1)} %copy.42, s32[4096]{0:T(1024)} %bitcast.146, bf16[128,4096]{0,1:T(8,128)(2,1)S(1)} %bitcast.132), kind=kCustom, calls=%fused_computation.20 | custom fusion | flops 1048576 | bytes 1572864 | tf_op jit(solution)/shard_map/scatter-add | solution.py:77
  498.8 1.0 copy.43
  (121 shorter events, 4.0 us)
Async XLA Ops:
  7.2 100.6 %copy-start = (bf16[128,128]{1,0:T(8,128)(2,1)S(1)}, bf16[128,128]{1,0:T(8,128)(2,1)}, u32[]{:S(2)}) copy-start(bf16[128,128]{1,0:T(8,128)(2,1)} %param.29) | copy-start | bytes 98308
  7.2 21.2 %all-to-all-start = ((s32[32,1,128]{2,1,0:T(1,128)}), s32[32,1,128]{2,1,0:T(1,128)S(1)}, u32[]{:S(2)}, u32[]{:S(2)}) async-start(s32[32,1,128]{2,1,0:T(1,128)} %bitcast.144), calls=%async_computation | async-start | bytes 32768 | tf_op jit(solution)/shard_map/all_to_all | solution.py:64
  40.6 6.8 %copy-start.38 = (s32[32]{0:T(128)S(1)}, s32[32]{0:T(128)}, u32[]{:S(2)}) copy-start(s32[32]{0:T(128)} %param.26) | copy-start | bytes 388
  40.6 6.9 %copy-start.8 = (bf16[128,4096]{1,0:T(8,128)(2,1)S(1)}, bf16[128,4096]{1,0:T(8,128)(2,1)}, u32[]{:S(2)}) copy-start(bf16[128,4096]{1,0:T(8,128)(2,1)} %param.22) | copy-start | bytes 3145732
  43.5 31.5 %all-to-all-start.1 = ((bf16[128,32,128]{0,2,1:T(8,128)(2,1)}), bf16[128,32,128]{0,2,1:T(8,128)(2,1)S(1)}, u32[]{:S(2)}, u32[]{:S(2)}) async-start(bf16[128,32,128]{0,2,1:T(8,128)(2,1)} %bitcast.6), calls=%async_computation.1 | async-start | bytes 2097152 | tf_op jit(solution)/shard_map/all_to_all | solution.py:70
  48.9 53.4 %copy-start.25 = (pred[4096]{0:T(1024)(128)(4,1)}, pred[4096]{0:T(1024)(128)(4,1)S(1)}, u32[]{:S(2)}) copy-start(pred[4096]{0:T(1024)(128)(4,1)S(1)} %compare_and_fusion) | copy-start | bytes 12292
  48.9 38.3 %copy-start.17 = (s32[4096]{0:T(1024)}, s32[4096]{0:T(1024)S(1)}, u32[]{:S(2)}) copy-start(s32[4096]{0:T(1024)S(1)} %fusion.50) | copy-start | bytes 49156
  49.6 62.2 %copy-start.21 = (s32[4096,1]{0,1:T(1,128)}, s32[4096,1]{0,1:T(1,128)S(1)}, u32[]{:S(2)}) copy-start(s32[4096,1]{0,1:T(1,128)S(1)} %get-tuple-element.26) | copy-start | bytes 49156
  102.3 3.1 copy-start.9
  102.3 3.1 copy-start.19
  102.3 3.1 copy-start.39
  105.4 2.4 copy-start.12
  105.4 2.3 copy-start.14
  107.7 1.0 copy-start.3
  107.7 1.8 copy-start.29
  107.7 1.8 copy-start.36
  108.2 1.3 copy-start.1
  136.2 32.8 %all-to-all-start.2 = ((bf16[128,32,128]{0,2,1:T(8,128)(2,1)}), bf16[128,32,128]{0,2,1:T(8,128)(2,1)}, u32[]{:S(2)}, u32[]{:S(2)}) async-start(bf16[128,32,128]{0,2,1:T(8,128)(2,1)} %bitcast.134), calls=%async_computation.2 | async-start | bytes 2097152 | tf_op jit(solution)/shard_map/all_to_all | solution.py:74
  141.3 50.8 %copy-start.40 = (f32[128]{0:T(128)S(1)}, f32[128]{0:T(128)}, u32[]{:S(2)}) copy-start(f32[128]{0:T(128)} %param.33) | copy-start | bytes 1540
  141.4 52.1 %copy-start.28 = (s32[4096,1]{0,1:T(1,128)}, s32[4096,1]{0,1:T(1,128)S(1)}, u32[]{:S(2)}) copy-start(s32[4096,1]{0,1:T(1,128)S(1)} %compare_select_fusion.1) | copy-start | bytes 49156
  192.1 1.3 copy-start.27
  192.1 1.6 copy-start.5
  192.2 1.6 copy-start.31
  192.2 2.4 copy-start.11
  192.2 2.4 copy-start.37
  194.6 1.9 copy-start.23
  196.5 21.0 %copy-start.6 = (bf16[128,1024]{0,1:T(8,128)(2,1)}, bf16[128,1024]{0,1:T(8,128)(2,1)S(1)}, u32[]{:S(2)}) copy-start(bf16[128,1024]{0,1:T(8,128)(2,1)S(1)} %get-tuple-element.39) | copy-start | bytes 786436
  211.7 32.6 %all-to-all-start.3 = ((bf16[128,32,128]{0,2,1:T(8,128)(2,1)}), bf16[128,32,128]{0,2,1:T(8,128)(2,1)S(1)}, u32[]{:S(2)}, u32[]{:S(2)}) async-start(bf16[128,32,128]{0,2,1:T(8,128)(2,1)} %bitcast.28), calls=%async_computation.3 | async-start | bytes 2097152 | tf_op jit(solution)/shard_map/all_to_all | solution.py:70
  216.7 257.5 %all-reduce.2.cloned.1.call-start = ((), (), s32[]{:S(2)}) async-start(), calls=%async_computation.5 | async-start | bytes 462848 | tf_op jit(solution)/shard_map/psum | solution.py:168
  217.4 27.0 %copy-start.18 = (s32[4096]{0:T(1024)S(1)}, s32[4096]{0:T(1024)}, u32[]{:S(2)}) copy-start(s32[4096]{0:T(1024)} %copy-done.17) | copy-start | bytes 49156
  259.5 1.9 copy-start.2
  261.4 2.5 copy-start.26
  261.4 2.5 copy-start.30
  263.8 1.2 copy-start.4
  265.1 1.6 copy-start.41
  266.7 1.5 copy-start.10
  266.7 1.5 copy-start.13
  266.7 1.9 copy-start.15
  268.5 1.4 copy-start.20
  274.8 23.3 %copy-start.22 = (s32[4096,1]{0,1:T(1,128)S(1)}, s32[4096,1]{0,1:T(1,128)}, u32[]{:S(2)}) copy-start(s32[4096,1]{0,1:T(1,128)} %copy-done.21) | copy-start | bytes 49156
  322.0 3.5 copy-start.35
  322.0 3.8 copy-start.34
  322.0 6.7 %copy-start.32 = (bf16[128]{0:T(256)(128)(2,1)S(1)}, bf16[128]{0:T(256)(128)(2,1)}, u32[]{:S(2)}) copy-start(bf16[128]{0:T(256)(128)(2,1)} %get-tuple-element.18) | copy-start | bytes 772
  322.0 7.0 %copy-start.33 = (bf16[128]{0:T(256)(128)(2,1)S(1)}, bf16[128]{0:T(256)(128)(2,1)}, u32[]{:S(2)}) copy-start(bf16[128]{0:T(256)(128)(2,1)} %reduce.4) | copy-start | bytes 772
  323.1 9.2 %copy-start.7 = (bf16[128,1024]{0,1:T(8,128)(2,1)S(1)}, bf16[128,1024]{0,1:T(8,128)(2,1)}, u32[]{:S(2)}) copy-start(bf16[128,1024]{0,1:T(8,128)(2,1)} %copy-done.6) | copy-start | bytes 786436
  323.1 9.2 %copy-start.24 = (bf16[128,256]{1,0:T(8,128)(2,1)S(1)}, bf16[128,256]{1,0:T(8,128)(2,1)}, u32[]{:S(2)}) copy-start(bf16[128,256]{1,0:T(8,128)(2,1)} %param.32) | copy-start | bytes 196612
  329.1 0.7 copy-start.16
  332.8 143.2 %all-to-all-start.4 = ((bf16[128,32,128]{0,2,1:T(8,128)(2,1)}), bf16[128,32,128]{0,2,1:T(8,128)(2,1)S(1)}, u32[]{:S(2)}, u32[]{:S(2)}) async-start(bf16[128,32,128]{0,2,1:T(8,128)(2,1)} %bitcast.32), calls=%async_computation.4 | async-start | bytes 2097152 | tf_op jit(solution)/shard_map/all_to_all | solution.py:74
Sparse Core Ops, SparseCore 0:
  330.0 144.1 all-reduce.1
where the time goes:
time: 508 us; the launch traced here: 507 us
  waiting for transfers between devices  222 us (44%)
  other arithmetic  136 us (27%)
  local copies, waits for them, and re-layouts  88.5 us (17%)
  starting transfers between devices  30.5 us (6%)
  matrix products  14.8 us (3%)
  between operations  14.8 us (3%)
    psum x1, waiting for transfers between devices, per_device(): lax.psum(jnp.concatenate([edge_vec, node_vec]).astype(jnp.bfloat16), 'cut')  136 us
    all_to_all x2, waiting for transfers between devices, fetch_mirrors(): lax.all_to_all(outgoing, 'cut', split_axis=1, concat_axis=1, tiled=True)  51.1 us
    scatter-add x2, other arithmetic, per_device(): grad_table = jnp.zeros((latent, local_width), jnp.float32).at[:, send_col...  47.1 us
    scatter-add x2, other arithmetic, reduce_mirrors(): result = master_part.at[:, mirror_index].add(returned)  45.9 us
    all_to_all x2, waiting for transfers between devices, reduce_mirrors(): lax.all_to_all(mirror_part.astype(jnp.bfloat16), 'cut', split_axis=1, con...  27.5 us
    gather x2, local copies, waits for them, and re-layouts, fetch_mirrors(): outgoing = jnp.take(master_part, mirror_index, axis=1)  24.3 us
    scatter-add x1, other arithmetic, per_device(): jnp.zeros((latent, local_width), jnp.float32).at[:, recv_cols].add(message)  23.3 us
    gather x2, local copies, waits for them, and re-layouts, per_device(): jnp.take(agg_table, recv_cols, axis=1).astype(jnp.float32)  16.7 us
  transfers between devices with their start and end apart: 6, of which 5 were waited for; matrix products, arithmetic and copies ran while one was open for 2% of the time, Pallas kernels for 0%

commit v1 on v0

--- a/solution.py
+++ b/solution.py
@@ -67,7 +67,12 @@
 
     def fetch_mirrors(master_part):
         outgoing = jnp.take(master_part, mirror_index, axis=1)
-        result = lax.all_to_all(outgoing, "cut", split_axis=1, concat_axis=1, tiled=True)
+        result = jnp.concatenate(
+            lax.all_to_all(
+                jnp.stack(jnp.split(outgoing, lax.axis_size("cut"), axis=1)), "cut", 0, 0
+            ),
+            axis=1,
+        )
         return result
 
     def reduce_mirrors(master_part, mirror_part):

time: 508 us -> 546 us (1.075)
  local copies, waits for them, and re-layouts: 88.5 us -> 128 us
    unnamed x99 -> x167, local copies, waits for them, and re-layouts: 14.8 us -> 53 us
where the time goes in v1:
time: 546 us; the launch traced here: 545 us
  waiting for transfers between devices  223 us (41%)
  other arithmetic  134 us (25%)
  local copies, waits for them, and re-layouts  128 us (23%)
  starting transfers between devices  30.7 us (6%)
  between operations  14.9 us (3%)
  matrix products  14.8 us (3%)
    psum x1, waiting for transfers between devices, per_device(): lax.psum(jnp.concatenate([edge_vec, node_vec]).astype(jnp.bfloat16), 'cut')  136 us
    unnamed x167, local copies, waits for them, and re-layouts  53 us
    all_to_all x2, waiting for transfers between devices, fetch_mirrors(): lax.all_to_all(jnp.stack(jnp.split(outgoing, lax.axis_size('cut'), axis=1...  51 us
    scatter-add x2, other arithmetic, per_device(): grad_table = jnp.zeros((latent, local_width), jnp.float32).at[:, send_col...  47.1 us
    scatter-add x2, other arithmetic, reduce_mirrors(): result = master_part.at[:, mirror_index].add(returned)  45.9 us
    all_to_all x2, waiting for transfers between devices, reduce_mirrors(): lax.all_to_all(mirror_part.astype(jnp.bfloat16), 'cut', split_axis=1, con...  27.5 us
    gather x2, local copies, waits for them, and re-layouts, fetch_mirrors(): outgoing = jnp.take(master_part, mirror_index, axis=1)  24.3 us
    scatter-add x1, other arithmetic, per_device(): jnp.zeros((latent, local_width), jnp.float32).at[:, recv_cols].add(message)  23.3 us
  transfers between devices with their start and end apart: 6, of which 5 were waited for; matrix products, arithmetic and copies ran while one was open for 2% of the time, Pallas kernels for 0%

profile of v1, /device:TPU:2, one launch (start us, length us, event | category | flops | bytes accessed | tf_op | source)
XLA Modules:
  0.0 545.3 jit_solution(9219302339278242080)
XLA Ops:
  7.2 11.5 %all-to-all-start = ((s32[32,1,128]{2,1,0:T(1,128)}), s32[32,1,128]{2,1,0:T(1,128)S(1)}, u32[]{:S(2)}, u32[]{:S(2)}) async-start(s32[32,1,128]{2,1,0:T(1,128)} %bitcast.402), calls=%async_computation | async-start | bytes 32768 | tf_op jit(solution)/shard_map/all_to_all | solution.py:64
  18.7 0.7 convert_bitcast_fusion.4
  19.4 1.1 copy.38
  20.5 7.9 %all-to-all-done = s32[32,1,128]{2,1,0:T(1,128)S(1)} async-done(((s32[32,1,128]{2,1,0:T(1,128)}), s32[32,1,128]{2,1,0:T(1,128)S(1)}, u32[]{:S(2)}, u32[]{:S(2)}) %all-to-all-start) | async-done | bytes 16416 | tf_op jit(solution)/shard_map/all_to_all | solution.py:64
  28.4 12.1 %gather_fusion = bf16[4096,128]{1,0:T(8,128)(2,1)S(1)} fusion(bf16[128,1024]{0,1:T(8,128)(2,1)S(1)} %copy.38, s32[4096]{0:T(1024)S(1)} %fusion.48), kind=kCustom, calls=%fused_computation.clone | custom fusion | bytes 2113536 | tf_op jit(solution)/shard_map/jit(_take)/gather | solution.py:69
  40.6 2.1 select_bitcast_fusion.3
  42.7 0.6 constant_dynamic-update-slice_fusion.31
  43.4 0.6 constant_dynamic-update-slice_fusion.30
  50.8 0.6 constant_dynamic-update-slice_fusion.18
  55.1 0.6 constant_dynamic-update-slice_fusion.11
  62.5 4.1 all-to-all-start.1
  66.7 1.3 copy.36
  68.2 0.6 compare_select_fusion
  68.9 25.3 %all-to-all-done.1 = bf16[32,128,128]{1,2,0:T(8,128)(2,1)S(1)} async-done(((bf16[32,128,128]{1,2,0:T(8,128)(2,1)}), bf16[32,128,128]{1,2,0:T(8,128)(2,1)S(1)}, u32[]{:S(2)}, u32[]{:S(2)}) %all-to-all-start.1) | async-done | bytes 1048608 | tf_op jit(solution)/shard_map/all_to_all | solution.py:71
  94.2 12.1 %gather_fusion.1 = bf16[4096,128]{1,0:T(8,128)(2,1)S(1)} fusion(bf16[128,5120]{0,1:T(8,128)(2,1)S(1)} %pad_maximum_fusion.1, s32[4096]{0:T(1024)S(1)} %get-tuple-element.40), kind=kCustom, calls=%fused_computation.1.clone | custom fusion | bytes 2113536 | tf_op jit(solution)/shard_map/jit(_take)/gather | solution.py:98
  106.4 15.0 %gather_fusion.2 = bf16[4096,128]{1,0:T(8,128)(2,1)} fusion(bf16[128,5120]{0,1:T(8,128)(2,1)S(1)} %pad_maximum_fusion.1, s32[4096]{0:T(1024)S(1)} %get-tuple-element.41), kind=kCustom, calls=%fused_computation.3.clone | custom fusion | bytes 2113536 | tf_op jit(solution)/shard_map/jit(_take)/gather | solution.py:99
  121.4 2.1 select_bitcast_fusion.2
  123.6 2.1 select_bitcast_fusion.1
  125.8 2.3 multiply_convert_fusion
  129.1 0.8 copy-done.1
  130.4 1.8 copy.37
  132.2 23.3 %scatter_custom_fusion = f32[128,5120]{0,1:T(8,128)S(1)} fusion(s32[4096]{0:T(1024)S(1)} %bitcast.400, f32[4096,128]{1,0:T(8,128)} %copy.37, f32[]{:T(128)} %constant.26.clone.1), kind=kCustom, calls=%fused_computation.47 | custom fusion | flops 524288 | bytes 2621952 | tf_op jit(solution)/shard_map/scatter-add | solution.py:108
  155.5 1.1 slice.89
  156.6 5.1 all-to-all-start.2
  161.8 27.5 %all-to-all-done.2 = bf16[128,32,128]{0,2,1:T(8,128)(2,1)} async-done(((bf16[128,32,128]{0,2,1:T(8,128)(2,1)}), bf16[128,32,128]{0,2,1:T(8,128)(2,1)}, u32[]{:S(2)}, u32[]{:S(2)}) %all-to-all-start.2) | async-done | bytes 1048608 | tf_op jit(solution)/shard_map/all_to_all | solution.py:79
  189.3 23.1 %scatter_custom_fusion.1 = f32[128,1024]{0,1:T(8,128)S(1)} fusion(f32[128,1024]{0,1:T(8,128)S(1)} %slice.66, s32[4096]{0:T(1024)S(1)} %bitcast.403, bf16[128,4096]{0,1:T(8,128)(2,1)} %bitcast.103), kind=kCustom, calls=%fused_computation.22 | custom fusion | flops 1048576 | bytes 1572864 | tf_op jit(solution)/shard_map/scatter-add | solution.py:82
  212.6 1.2 multiply_convert_fusion.1
  214.2 0.8 fusion.37
  215.0 1.0 fusion.35
  215.9 0.8 fusion.62
  217.0 12.1 %gather_fusion.3 = bf16[4096,128]{1,0:T(8,128)(2,1)S(1)} fusion(bf16[128,1024]{0,1:T(8,128)(2,1)S(1)} %fusion.25, s32[4096]{0:T(1024)S(1)} %fusion.48), kind=kCustom, calls=%fused_computation.2.clone | custom fusion | bytes 2113536 | tf_op jit(solution)/shard_map/jit(_take)/gather | solution.py:69
  229.1 2.1 select_bitcast_fusion
  231.3 0.6 constant_dynamic-update-slice_fusion.63
  238.1 0.6 constant_dynamic-update-slice_fusion.52
  251.0 5.0 all-to-all-start.3
  256.1 0.7 reduce.4
  257.1 0.8 fusion.29
  257.9 25.7 %all-to-all-done.3 = bf16[32,128,128]{1,2,0:T(8,128)(2,1)S(1)} async-done(((bf16[32,128,128]{1,2,0:T(8,128)(2,1)}), bf16[32,128,128]{1,2,0:T(8,128)(2,1)S(1)}, u32[]{:S(2)}, u32[]{:S(2)}) %all-to-all-start.3) | async-done | bytes 1048608 | tf_op jit(solution)/shard_map/all_to_all | solution.py:71
  283.8 15.0 %gather_fusion.4 = bf16[4096,128]{1,0:T(8,128)(2,1)} fusion(bf16[128,5120]{0,1:T(8,128)(2,1)S(1)} %pad_maximum_fusion.2, s32[4096]{0:T(1024)S(1)} %copy-done.20), kind=kCustom, calls=%fused_computation.4.clone | custom fusion | bytes 2113536 | tf_op jit(solution)/shard_map/jit(_take)/gather | solution.py:142
  298.8 1.6 copy.40
  300.7 1.7 fusion.12
  302.5 0.7 fusion.11
  304.1 1.2 copy-done.44
  305.3 1.5 fusion.58
  307.1 1.4 fusion.26
  308.5 1.4 fusion.2
  309.9 1.8 fusion.42
  311.7 1.7 fusion.44
  313.4 23.3 %scatter_custom_fusion.2 = f32[128,5120]{0,1:T(8,128)S(1)} fusion(s32[4096]{0:T(1024)} %bitcast.405, f32[4096,128]{1,0:T(8,128)} %fusion.44, f32[]{:T(128)} %constant.26.clone.1), kind=kCustom, calls=%fused_computation.45 | custom fusion | flops 524288 | bytes 2621952 | tf_op jit(solution)/shard_map/scatter-add | solution.py:157
  336.7 23.8 %scatter_fusion = f32[128,5120]{0,1:T(8,128)S(1)} fusion(f32[128,5120]{0,1:T(8,128)S(1)} %scatter_custom_fusion.2, s32[4096]{0:T(1024)S(1)} %bitcast.401, f32[4096,128]{1,0:T(8,128)} %fusion.42), kind=kCustom, calls=%fused_computation.8 | custom fusion | flops 524288 | bytes 6307840 | tf_op jit(solution)/shard_map/scatter-add | solution.py:159
  360.6 1.1 slice.88
  361.7 1.0 reshape.219
  362.7 0.8 dynamic-update-slice.1
  364.6 0.8 dynamic-update-slice.5
  365.4 0.8 dynamic-update-slice.6
  366.2 1.1 dynamic-update-slice.7
  367.7 0.7 copy-done.18
  368.4 2.3 copy.44
  371.4 5.0 all-to-all-start.4
  376.4 136.5 %all-reduce.2.cloned.1.call-done = bf16[115456]{0:T(1024)(128)(2,1)} async-done(((bf16[115456]{0:T(1024)(128)(2,1)}), bf16[115456]{0:T(1024)(128)(2,1)}) %all-reduce.2.cloned.1.call-update) | async-done | bytes 230928 | tf_op jit(solution)/shard_map/psum | solution.py:173
  512.8 1.0 convert_element_type.94
  513.9 0.8 pad_maximum_fusion.8
  514.7 22.7 %scatter_custom_fusion.4 = f32[128,1024]{0,1:T(8,128)S(1)} fusion(f32[128,1024]{0,1:T(8,128)S(1)} %copy.42, s32[4096]{0:T(1024)} %bitcast.404, bf16[128,4096]{0,1:T(8,128)(2,1)S(1)} %bitcast.390), kind=kCustom, calls=%fused_computation.20 | custom fusion | flops 1048576 | bytes 1572864 | tf_op jit(solution)/shard_map/scatter-add | solution.py:82
  537.4 1.0 copy.43
  (191 shorter events, 42.4 us)
Async XLA Ops:
  7.2 120.9 %copy-start = (bf16[128,128]{1,0:T(8,128)(2,1)S(1)}, bf16[128,128]{1,0:T(8,128)(2,1)}, u32[]{:S(2)}) copy-start(bf16[128,128]{1,0:T(8,128)(2,1)} %param.29) | copy-start | bytes 98308
  7.2 21.2 %all-to-all-start = ((s32[32,1,128]{2,1,0:T(1,128)}), s32[32,1,128]{2,1,0:T(1,128)S(1)}, u32[]{:S(2)}, u32[]{:S(2)}) async-start(s32[32,1,128]{2,1,0:T(1,128)} %bitcast.402), calls=%async_computation | async-start | bytes 32768 | tf_op jit(solution)/shard_map/all_to_all | solution.py:64
  42.7 23.9 %copy-start.39 = (s32[32,2]{0,1:T(2,128)S(1)}, s32[32,2]{0,1:T(2,128)}, u32[]{:S(2)}) copy-start(s32[32,2]{0,1:T(2,128)} %param.24) | copy-start | bytes 772
  42.7 24.0 %copy-start.10 = (bf16[128,4096]{1,0:T(8,128)(2,1)S(1)}, bf16[128,4096]{1,0:T(8,128)(2,1)}, u32[]{:S(2)}) copy-start(bf16[128,4096]{1,0:T(8,128)(2,1)} %param.22) | copy-start | bytes 3145732
  62.5 5.5 %copy-start.30 = (s32[32,2,128]{2,1,0:T(2,128)S(1)}, s32[32,2,128]{2,1,0:T(2,128)}, u32[]{:S(2)}) copy-start(s32[32,2,128]{2,1,0:T(2,128)} %param.25) | copy-start | bytes 98308
  62.5 31.6 %all-to-all-start.1 = ((bf16[32,128,128]{1,2,0:T(8,128)(2,1)}), bf16[32,128,128]{1,2,0:T(8,128)(2,1)S(1)}, u32[]{:S(2)}, u32[]{:S(2)}) async-start(bf16[32,128,128]{1,2,0:T(8,128)(2,1)} %constant_dynamic-update-slice_fusion), calls=%async_computation.1 | async-start | bytes 2097152 | tf_op jit(solution)/shard_map/all_to_all | solution.py:71
  68.2 55.4 %copy-start.27 = (pred[4096]{0:T(1024)(128)(4,1)}, pred[4096]{0:T(1024)(128)(4,1)S(1)}, u32[]{:S(2)}) copy-start(pred[4096]{0:T(1024)(128)(4,1)S(1)} %compare_and_fusion) | copy-start | bytes 12292
  68.2 38.2 %copy-start.19 = (s32[4096]{0:T(1024)}, s32[4096]{0:T(1024)S(1)}, u32[]{:S(2)}) copy-start(s32[4096]{0:T(1024)S(1)} %get-tuple-element.41) | copy-start | bytes 49156
  68.8 63.4 %copy-start.23 = (s32[4096,1]{0,1:T(1,128)}, s32[4096,1]{0,1:T(1,128)S(1)}, u32[]{:S(2)}) copy-start(s32[4096,1]{0,1:T(1,128)S(1)} %get-tuple-element.26) | copy-start | bytes 49156
  121.4 2.2 copy-start.5
  121.4 4.4 copy-start.11
  121.4 4.4 copy-start.21
  121.4 4.4 copy-start.42
  123.6 4.5 copy-start.13
  125.8 2.3 copy-start.15
  128.1 1.0 copy-start.3
  128.1 1.8 copy-start.32
  128.1 1.8 copy-start.40
  128.6 1.3 copy-start.1
  156.6 32.7 %all-to-all-start.2 = ((bf16[128,32,128]{0,2,1:T(8,128)(2,1)}), bf16[128,32,128]{0,2,1:T(8,128)(2,1)}, u32[]{:S(2)}, u32[]{:S(2)}) async-start(bf16[128,32,128]{0,2,1:T(8,128)(2,1)} %bitcast.392), calls=%async_computation.2 | async-start | bytes 2097152 | tf_op jit(solution)/shard_map/all_to_all | solution.py:79
  161.7 50.8 %copy-start.43 = (f32[128]{0:T(128)S(1)}, f32[128]{0:T(128)}, u32[]{:S(2)}) copy-start(f32[128]{0:T(128)} %param.33) | copy-start | bytes 1540
  161.8 52.0 %copy-start.31 = (s32[4096,1]{0,1:T(1,128)}, s32[4096,1]{0,1:T(1,128)S(1)}, u32[]{:S(2)}) copy-start(s32[4096,1]{0,1:T(1,128)S(1)} %compare_select_fusion.1) | copy-start | bytes 49156
  212.5 1.3 copy-start.29
  212.5 1.6 copy-start.6
  212.5 1.6 copy-start.34
  212.6 2.4 copy-start.17
  212.6 2.4 copy-start.41
  214.9 1.8 copy-start.25
  216.8 40.0 %copy-start.8 = (bf16[128,1024]{0,1:T(8,128)(2,1)}, bf16[128,1024]{0,1:T(8,128)(2,1)S(1)}, u32[]{:S(2)}) copy-start(bf16[128,1024]{0,1:T(8,128)(2,1)S(1)} %get-tuple-element.39) | copy-start | bytes 786436
  251.0 32.6 %all-to-all-start.3 = ((bf16[32,128,128]{1,2,0:T(8,128)(2,1)}), bf16[32,128,128]{1,2,0:T(8,128)(2,1)S(1)}, u32[]{:S(2)}, u32[]{:S(2)}) async-start(bf16[32,128,128]{1,2,0:T(8,128)(2,1)} %constant_dynamic-update-slice_fusion.32), calls=%async_computation.3 | async-start | bytes 2097152 | tf_op jit(solution)/shard_map/all_to_all | solution.py:71
  256.0 256.8 %all-reduce.2.cloned.1.call-start = ((), (), s32[]{:S(2)}) async-start(), calls=%async_computation.5 | async-start | bytes 462848 | tf_op jit(solution)/shard_map/psum | solution.py:173
  256.7 27.0 %copy-start.20 = (s32[4096]{0:T(1024)S(1)}, s32[4096]{0:T(1024)}, u32[]{:S(2)}) copy-start(s32[4096]{0:T(1024)} %copy-done.19) | copy-start | bytes 49156
  283.7 16.7 %copy-start.28 = (pred[4096]{0:T(1024)(128)(4,1)S(1)}, pred[4096]{0:T(1024)(128)(4,1)}, u32[]{:S(2)}) copy-start(pred[4096]{0:T(1024)(128)(4,1)} %copy-done.27) | copy-start | bytes 12292
  283.8 16.7 %copy-start.33 = (f32[128]{0:T(128)S(1)}, f32[128]{0:T(128)}, u32[]{:S(2)}) copy-start(f32[128]{0:T(128)} %param.30) | copy-start | bytes 1540
  298.8 1.9 copy-start.2
  302.5 1.2 copy-start.4
  303.7 1.6 copy-start.44
  305.3 1.5 copy-start.12
  305.3 1.5 copy-start.14
  305.3 1.9 copy-start.16
  307.1 1.4 copy-start.22
  313.4 23.3 %copy-start.24 = (s32[4096,1]{0,1:T(1,128)S(1)}, s32[4096,1]{0,1:T(1,128)}, u32[]{:S(2)}) copy-start(s32[4096,1]{0,1:T(1,128)} %copy-done.23) | copy-start | bytes 49156
  360.5 3.5 copy-start.38
  360.6 3.8 copy-start.37
  360.6 6.7 %copy-start.35 = (bf16[128]{0:T(256)(128)(2,1)S(1)}, bf16[128]{0:T(256)(128)(2,1)}, u32[]{:S(2)}) copy-start(bf16[128]{0:T(256)(128)(2,1)} %get-tuple-element.18) | copy-start | bytes 772
  360.6 6.9 %copy-start.36 = (bf16[128]{0:T(256)(128)(2,1)S(1)}, bf16[128]{0:T(256)(128)(2,1)}, u32[]{:S(2)}) copy-start(bf16[128]{0:T(256)(128)(2,1)} %reduce.4) | copy-start | bytes 772
  361.7 9.2 %copy-start.7 = (bf16[128,1024]{1,0:T(8,128)(2,1)S(1)}, bf16[128,1024]{1,0:T(8,128)(2,1)}, u32[]{:S(2)}) copy-start(bf16[128,1024]{1,0:T(8,128)(2,1)} %param.37) | copy-start | bytes 786436
  361.7 9.2 %copy-start.9 = (bf16[128,1024]{0,1:T(8,128)(2,1)S(1)}, bf16[128,1024]{0,1:T(8,128)(2,1)}, u32[]{:S(2)}) copy-start(bf16[128,1024]{0,1:T(8,128)(2,1)} %copy-done.8) | copy-start | bytes 786436
  361.7 9.2 %copy-start.26 = (bf16[128,256]{1,0:T(8,128)(2,1)S(1)}, bf16[128,256]{1,0:T(8,128)(2,1)}, u32[]{:S(2)}) copy-start(bf16[128,256]{1,0:T(8,128)(2,1)} %param.32) | copy-start | bytes 196612
  367.7 0.7 copy-start.18
  371.4 143.3 %all-to-all-start.4 = ((bf16[128,32,128]{0,2,1:T(8,128)(2,1)}), bf16[128,32,128]{0,2,1:T(8,128)(2,1)S(1)}, u32[]{:S(2)}, u32[]{:S(2)}) async-start(bf16[128,32,128]{0,2,1:T(8,128)(2,1)} %bitcast.96), calls=%async_computation.4 | async-start | bytes 2097152 | tf_op jit(solution)/shard_map/all_to_all | solution.py:79
Sparse Core Ops, SparseCore 0:
  368.5 144.2 all-reduce.1
